TPU v7x, 512 devices: a whole 4x4x16 slice. The times are simulated.
512 devices in a mesh: blk: 64 (over x, z), grp: 8 (over y, core).
Axes of the slice: x: 4, y: 4, z: 16, core: 2. Of those that a mesh axis runs over, the one named last changes fastest.
Arguments:
- points: bfloat16 [8, 65536, 128], P('grp', 'blk'), may hold values from -4 to 4
- start_panel: bfloat16 [8, 64, 65536], P('grp', None, 'blk'), may hold values from -6 to 6
- seventh: int32 [8, 65536], P('grp', 'blk'), may hold values from 0 to 255, as said below
- neighbours: int32 [8, 256, 16], P('grp'), may hold values from 0 to 255, as said below
- counts: int32 [8, 256], P('grp'), may hold values from 1 to 16, as said below
Outputs:
- ortho_basis: float32 [8, 64, 65536], P('grp', None, 'blk')
- r_factor: float32 [64, 64], replicated
Inputs may be any that keep to these rules, and one draw needn't show every extreme that they name: `seventh`: A point's position within its own block, never the point's own position. `neighbours`: block numbers within the group; block B's owner is B // 4. The listed entries of a block are distinct, never the block itself, and each is owned by an owner whose number differs from B's owner by at most 4 modulo 64. The entries after the listed ones are block numbers of the group and are not used. Of the blocks of one owner, at most 2 are listed by the blocks of another owner together, and exactly 2 for some pairs of owners. `counts`: some block of every group lists 16 blocks.
All inputs are finite; a program needn't handle non-finite values.
Results may differ from a plain program's by a relative error of at most 0.0082.
Values may be sent and summed in bfloat16 or wider, within the bound.
A program may use at most 64 MiB of HBM per device.

v0:
```python
import math
import jax
import jax.numpy as jnp
from jax import lax
from jax.sharding import PartitionSpec as P

E = 128
K = 64
BS = 256
SLOTS = 16
REACH = 4


def passed_along(block, axis, distance):
    devices = range(lax.axis_size(axis))
    route = [((i - distance) % len(devices), i) for i in devices]
    return lax.ppermute(block, axis, route)


def fetch_whole(send_points, send_panel, send_scales, offset):
    return passed_along((send_points, send_panel, send_scales), "blk", offset)


def tile_terms(
    row_points, row_scales, row_norms, col_points, col_panel, col_scales, col_norms, pair_mask
):
    inner_prod = jnp.einsum(
        "pe,cqe->cpq", row_points, col_points, preferred_element_type=jnp.float32
    )
    distance = row_norms[None, :, None] + col_norms[:, None, :] - 2.0 * inner_prod
    denom_scale = (
        row_scales.astype(jnp.float32)[None, :, None] * col_scales.astype(jnp.float32)[:, None, :]
    )
    affinity = jnp.exp(-distance / denom_scale) * pair_mask[:, None, None]
    weights = affinity.astype(jnp.bfloat16)
    carried = jnp.einsum("cpq,kcq->kp", weights, col_panel, preferred_element_type=jnp.float32)
    return (carried, jnp.sum(affinity, axis=(0, 2)))


def local(points, start_panel, seventh, neighbours, counts):
    cycle_size = lax.axis_size("blk")
    my_index = lax.axis_index("blk")
    per_dev = points.shape[1] // BS
    own_points = points[0].reshape(per_dev, BS, E)
    partner_pos = seventh[0].reshape(per_dev, BS)
    partner = jnp.take_along_axis(own_points, partner_pos[:, :, None], axis=1)
    difference = own_points.astype(jnp.float32) - partner.astype(jnp.float32)
    scales = jnp.sqrt(jnp.sum(difference * difference, axis=-1) + 1e-06).astype(jnp.bfloat16)
    as_float = own_points.astype(jnp.float32)
    sq_norm = jnp.sum(as_float * as_float, axis=-1)
    own_panel = start_panel[0].reshape(K, per_dev, BS)
    block_lists = neighbours[0]
    live_mask = jnp.arange(SLOTS, dtype=jnp.int32)[None, :] < counts[0][:, None]
    my_lists = lax.dynamic_slice_in_dim(block_lists, my_index * per_dev, per_dev, 0)
    my_live = lax.dynamic_slice_in_dim(live_mask, my_index * per_dev, per_dev, 0)

    def accumulate(totals, col_points, col_panel, col_scales, col_ids):
        pair_mask = jnp.any(
            (my_lists[:, :, None] == col_ids[None, None, :]) & my_live[:, :, None], axis=1
        ).astype(jnp.float32)
        col_float = col_points.astype(jnp.float32)
        col_norms = jnp.sum(col_float * col_float, axis=-1)

        def per_block(inputs):
            row_points, row_scales, row_norms, row_mask = inputs
            return tile_terms(
                row_points,
                row_scales,
                row_norms,
                col_points,
                col_panel,
                col_scales,
                col_norms,
                row_mask,
            )

        carried, degree = lax.map(per_block, (own_points, scales, sq_norm, pair_mask))
        return (totals[0] + carried, totals[1] + degree)

    totals = (jnp.zeros((per_dev, K, BS), jnp.float32), jnp.zeros((per_dev, BS), jnp.float32))
    local_ids = my_index * per_dev + jnp.arange(per_dev, dtype=jnp.int32)
    totals = accumulate(totals, own_points, own_panel, scales, local_ids)
    for offset in list(range(1, REACH + 1)) + list(range(-REACH, 0)):
        source = (my_index - offset) % cycle_size
        col_points, col_panel, col_scales = fetch_whole(own_points, own_panel, scales, offset)
        col_ids = source * per_dev + jnp.arange(per_dev, dtype=jnp.int32)
        totals = accumulate(totals, col_points, col_panel, col_scales, col_ids)
    carried = jnp.transpose(totals[0], (1, 0, 2))
    degree = 1.0 + totals[1]
    walked = ((own_panel.astype(jnp.float32) + carried) / degree[None, :, :]).reshape(
        K, per_dev * BS
    )
    gram_local = jnp.dot(
        walked, walked.T, precision=lax.Precision.HIGHEST, preferred_element_type=jnp.float32
    )
    gram_matrix = lax.psum(gram_local, ("blk", "grp"))
    lower_factor = jnp.linalg.cholesky(gram_matrix)
    solved = lax.linalg.triangular_solve(lower_factor, walked, left_side=True, lower=True)
    point_total = points.shape[1] * lax.axis_size("blk") * lax.axis_size("grp")
    root_count = math.sqrt(point_total)
    ortho_basis = (solved * root_count)[None]
    r_factor = lower_factor.T / root_count
    return (ortho_basis, r_factor)


def solution(mesh):
    in_specs = (
        P("grp", "blk", None),
        P("grp", None, "blk"),
        P("grp", "blk"),
        P("grp", None, None),
        P("grp", None),
    )
    out_specs = (P("grp", None, "blk"), P())
    return jax.shard_map(local, mesh=mesh, in_specs=in_specs, out_specs=out_specs, check_vma=False)
```

profile of v0, /device:TPU:1, one launch (start us, length us, event | category | flops | bytes accessed | tf_op | source)
XLA Modules:
  0.0 331.3 jit_solution(13664249299728064872)
XLA Ops:
  1.6 4.4 %collective-permute-start.2 = (bf16[64,4,256]{2,1,0:T(4,128)(2,1)S(1)}, bf16[64,4,256]{2,1,0:T(4,128)(2,1)S(1)}, u32[]{:S(2)}, u32[]{:S(2)}) collective-permute-start(bf16[64,4,256]{2,1,0:T(4,128)(2,1)S(1)} %reshape_squeeze.6), channel_id=1, source_target_pairs={{504,0},{0,8},{8,16},{16,24},{24,32},{32,40},{40,48},{48,56},{56,6... | collective-permute-start | bytes 393224 | tf_op jit(solution)/shard_map/ppermute | solution.py:17
  6.0 4.9 %collective-permute-start.5 = (bf16[64,4,256]{2,1,0:T(4,128)(2,1)S(1)}, bf16[64,4,256]{2,1,0:T(4,128)(2,1)S(1)}, u32[]{:S(2)}, u32[]{:S(2)}) collective-permute-start(bf16[64,4,256]{2,1,0:T(4,128)(2,1)S(1)} %reshape_squeeze.6), channel_id=1, source_target_pairs={{496,0},{504,8},{0,16},{8,24},{16,32},{24,40},{32,48},{40,56},{48,... | collective-permute-start | bytes 393224 | tf_op jit(solution)/shard_map/ppermute | solution.py:17
  10.9 7.5 %collective-permute-start.8 = (bf16[64,4,256]{2,1,0:T(4,128)(2,1)S(1)}, bf16[64,4,256]{2,1,0:T(4,128)(2,1)S(1)}, u32[]{:S(2)}, u32[]{:S(2)}) collective-permute-start(bf16[64,4,256]{2,1,0:T(4,128)(2,1)S(1)} %reshape_squeeze.6), channel_id=1, source_target_pairs={{488,0},{496,8},{504,16},{0,24},{8,32},{16,40},{24,48},{32,56},{40... | collective-permute-start | bytes 393224 | tf_op jit(solution)/shard_map/ppermute | solution.py:17
  18.4 7.0 %collective-permute-start.11 = (bf16[64,4,256]{2,1,0:T(4,128)(2,1)S(1)}, bf16[64,4,256]{2,1,0:T(4,128)(2,1)S(1)}, u32[]{:S(2)}, u32[]{:S(2)}) collective-permute-start(bf16[64,4,256]{2,1,0:T(4,128)(2,1)S(1)} %reshape_squeeze.6), channel_id=1, source_target_pairs={{480,0},{488,8},{496,16},{504,24},{0,32},{8,40},{16,48},{24,56},{3... | collective-permute-start | bytes 393224 | tf_op jit(solution)/shard_map/ppermute | solution.py:17
  25.4 2.6 collective-permute-start
  30.2 6.8 %gather_fusion = bf16[1024,128]{1,0:T(8,128)(2,1)S(1)} fusion(bf16[4,256,128]{2,1,0:T(8,128)(2,1)} %bitcast.90, s32[1024]{0:T(1024)S(1)} %bitcast.504), kind=kCustom, calls=%fused_computation | custom fusion | bytes 532480 | tf_op jit(solution)/shard_map/jit(take_along_axis)/gather | solution.py:46
  40.1 5.2 %collective-permute-start.14 = (bf16[64,4,256]{2,1,0:T(4,128)(2,1)S(1)}, bf16[64,4,256]{2,1,0:T(4,128)(2,1)S(1)}, u32[]{:S(2)}, u32[]{:S(2)}) collective-permute-start(bf16[64,4,256]{2,1,0:T(4,128)(2,1)S(1)} %reshape_squeeze.6), channel_id=1, source_target_pairs={{32,0},{40,8},{48,16},{56,24},{64,32},{72,40},{80,48},{88,56},{96,... | collective-permute-start | bytes 393224 | tf_op jit(solution)/shard_map/ppermute | solution.py:17
  45.3 3.6 %collective-permute-start.17 = (bf16[64,4,256]{2,1,0:T(4,128)(2,1)S(1)}, bf16[64,4,256]{2,1,0:T(4,128)(2,1)S(1)}, u32[]{:S(2)}, u32[]{:S(2)}) collective-permute-start(bf16[64,4,256]{2,1,0:T(4,128)(2,1)S(1)} %reshape_squeeze.6), channel_id=1, source_target_pairs={{24,0},{32,8},{40,16},{48,24},{56,32},{64,40},{72,48},{80,56},{88,... | collective-permute-start | bytes 393224 | tf_op jit(solution)/shard_map/ppermute | solution.py:17
  48.9 3.7 %collective-permute-start.20 = (bf16[64,4,256]{2,1,0:T(4,128)(2,1)S(1)}, bf16[64,4,256]{2,1,0:T(4,128)(2,1)S(1)}, u32[]{:S(2)}, u32[]{:S(2)}) collective-permute-start(bf16[64,4,256]{2,1,0:T(4,128)(2,1)S(1)} %reshape_squeeze.6), channel_id=1, source_target_pairs={{16,0},{24,8},{32,16},{40,24},{48,32},{56,40},{64,48},{72,56},{80,... | collective-permute-start | bytes 393224 | tf_op jit(solution)/shard_map/ppermute | solution.py:17
  52.5 3.1 collective-permute-start.23
  55.7 13.1 %while.109 = (s32[]{:T(128)}, f32[4,64,256]{2,1,0:T(8,128)S(1)}, f32[4,256]{1,0:T(4,128)S(1)}, f32[4,256]{1,0:T(4,128)S(1)}, bf16[4,256,128]{2,1,0:T(8,128)(2,1)...) while((s32[]{:T(128)}, f32[4,64,256]{2,1,0:T(8,128)S(1)}, ...), condition=%wide.region_5.6_spmd, body=%wide.region_3.0_spmd.sunk | while | flops 103023616 | bytes 1596585 | solution.py:77
  71.2 2.5 collective-permute-start.4
  73.7 5.2 %collective-permute-start.3 = (bf16[4,256,128]{2,1,0:T(8,128)(2,1)}, bf16[4,256,128]{2,1,0:T(8,128)(2,1)S(1)}, u32[]{:S(2)}, u32[]{:S(2)}) collective-permute-start(bf16[4,256,128]{2,1,0:T(8,128)(2,1)} %bitcast.90), channel_id=1, source_target_pairs={{496,0},{504,8},{0,16},{8,24},{16,32},{24,40},{32,48},{40,56},{48,... | collective-permute-start | bytes 786440 | tf_op jit(solution)/shard_map/ppermute | solution.py:17
  79.0 5.9 %collective-permute-start.7 = (bf16[4,256]{1,0:T(4,128)(2,1)}, bf16[4,256]{1,0:T(4,128)(2,1)S(1)}, u32[]{:S(2)}, u32[]{:S(2)}) collective-permute-start(bf16[4,256]{1,0:T(4,128)(2,1)} %convert_element_type.264), channel_id=1, source_target_pairs={{488,0},{496,8},{504,16},{0,24},{8,32},{16,40},{24,48},{32,56},{40... | collective-permute-start | bytes 6152 | tf_op jit(solution)/shard_map/ppermute | solution.py:17
  85.0 2.4 collective-permute-start.6
  89.5 9.6 %while.110 = (s32[]{:T(128)}, f32[4,64,256]{2,1,0:T(8,128)S(1)}, f32[4,256]{1,0:T(4,128)S(1)}, f32[4,256]{1,0:T(4,128)S(1)}, f32[4,256]{1,0:T(4,128)S(1)}, /*ind...) while((s32[]{:T(128)}, f32[4,64,256]{2,1,0:T(8,128)S(1)}, ...), condition=%wide.region_10.11_spmd, body=%wide.region_8.10_spmd.sunk | while | flops 103023616 | bytes 1596609 | solution.py:77
  99.2 4.9 %collective-permute-start.9 = (bf16[4,256,128]{2,1,0:T(8,128)(2,1)}, bf16[4,256,128]{2,1,0:T(8,128)(2,1)S(1)}, u32[]{:S(2)}, u32[]{:S(2)}) collective-permute-start(bf16[4,256,128]{2,1,0:T(8,128)(2,1)} %bitcast.90), channel_id=1, source_target_pairs={{480,0},{488,8},{496,16},{504,24},{0,32},{8,40},{16,48},{24,56},{3... | collective-permute-start | bytes 786440 | tf_op jit(solution)/shard_map/ppermute | solution.py:17
  104.3 6.4 %collective-permute-start.13 = (bf16[4,256]{1,0:T(4,128)(2,1)}, bf16[4,256]{1,0:T(4,128)(2,1)S(1)}, u32[]{:S(2)}, u32[]{:S(2)}) collective-permute-start(bf16[4,256]{1,0:T(4,128)(2,1)} %convert_element_type.264), channel_id=1, source_target_pairs={{32,0},{40,8},{48,16},{56,24},{64,32},{72,40},{80,48},{88,56},{96,... | collective-permute-start | bytes 6152 | tf_op jit(solution)/shard_map/ppermute | solution.py:17
  110.8 9.6 %while.111 = (s32[]{:T(128)}, f32[4,64,256]{2,1,0:T(8,128)S(1)}, f32[4,256]{1,0:T(4,128)S(1)}, f32[4,256]{1,0:T(4,128)S(1)}, f32[4,256]{1,0:T(4,128)S(1)}, /*ind...) while((s32[]{:T(128)}, f32[4,64,256]{2,1,0:T(8,128)S(1)}, ...), condition=%wide.region_15.16_spmd, body=%wide.region_13.15_spmd.sunk | while | flops 103023616 | bytes 1596609 | solution.py:77
  120.4 7.3 %collective-permute-start.12 = (bf16[4,256,128]{2,1,0:T(8,128)(2,1)}, bf16[4,256,128]{2,1,0:T(8,128)(2,1)S(1)}, u32[]{:S(2)}, u32[]{:S(2)}) collective-permute-start(bf16[4,256,128]{2,1,0:T(8,128)(2,1)} %bitcast.90), channel_id=1, source_target_pairs={{32,0},{40,8},{48,16},{56,24},{64,32},{72,40},{80,48},{88,56},{96,... | collective-permute-start | bytes 786440 | tf_op jit(solution)/shard_map/ppermute | solution.py:17
  127.9 5.9 %collective-permute-start.16 = (bf16[4,256]{1,0:T(4,128)(2,1)}, bf16[4,256]{1,0:T(4,128)(2,1)S(1)}, u32[]{:S(2)}, u32[]{:S(2)}) collective-permute-start(bf16[4,256]{1,0:T(4,128)(2,1)} %convert_element_type.264), channel_id=1, source_target_pairs={{24,0},{32,8},{40,16},{48,24},{56,32},{64,40},{72,48},{80,56},{88,... | collective-permute-start | bytes 6152 | tf_op jit(solution)/shard_map/ppermute | solution.py:17
  133.9 9.6 %while.112 = (s32[]{:T(128)}, f32[4,64,256]{2,1,0:T(8,128)S(1)}, f32[4,256]{1,0:T(4,128)S(1)}, f32[4,256]{1,0:T(4,128)S(1)}, f32[4,256]{1,0:T(4,128)S(1)}, /*ind...) while((s32[]{:T(128)}, f32[4,64,256]{2,1,0:T(8,128)S(1)}, ...), condition=%wide.region_20.21_spmd, body=%wide.region_18.20_spmd.sunk | while | flops 103023616 | bytes 1596609 | solution.py:77
  148.1 9.6 %while.113 = (s32[]{:T(128)}, f32[4,64,256]{2,1,0:T(8,128)S(1)}, f32[4,256]{1,0:T(4,128)S(1)}, f32[4,256]{1,0:T(4,128)S(1)}, f32[4,256]{1,0:T(4,128)S(1)}, /*ind...) while((s32[]{:T(128)}, f32[4,64,256]{2,1,0:T(8,128)S(1)}, ...), condition=%wide.region_25.26_spmd, body=%wide.region_23.25_spmd.sunk | while | flops 103023616 | bytes 1596609 | solution.py:77
  157.7 4.8 %collective-permute-start.18 = (bf16[4,256,128]{2,1,0:T(8,128)(2,1)}, bf16[4,256,128]{2,1,0:T(8,128)(2,1)S(1)}, u32[]{:S(2)}, u32[]{:S(2)}) collective-permute-start(bf16[4,256,128]{2,1,0:T(8,128)(2,1)} %bitcast.90), channel_id=1, source_target_pairs={{16,0},{24,8},{32,16},{40,24},{48,32},{56,40},{64,48},{72,56},{80,... | collective-permute-start | bytes 786440 | tf_op jit(solution)/shard_map/ppermute | solution.py:17
  162.8 3.1 collective-permute-start.22
  165.9 9.6 %while.114 = (s32[]{:T(128)}, f32[4,64,256]{2,1,0:T(8,128)S(1)}, f32[4,256]{1,0:T(4,128)S(1)}, f32[4,256]{1,0:T(4,128)S(1)}, f32[4,256]{1,0:T(4,128)S(1)}, /*ind...) while((s32[]{:T(128)}, f32[4,64,256]{2,1,0:T(8,128)S(1)}, ...), condition=%wide.region_30.31_spmd, body=%wide.region_28.30_spmd.sunk | while | flops 103023616 | bytes 1596609 | solution.py:77
  177.9 9.6 %while.115 = (s32[]{:T(128)}, f32[4,64,256]{2,1,0:T(8,128)S(1)}, f32[4,256]{1,0:T(4,128)S(1)}, f32[4,256]{1,0:T(4,128)S(1)}, f32[4,256]{1,0:T(4,128)S(1)}, /*ind...) while((s32[]{:T(128)}, f32[4,64,256]{2,1,0:T(8,128)S(1)}, ...), condition=%wide.region_35.36_spmd, body=%wide.region_33.35_spmd.sunk | while | flops 103023616 | bytes 1596609 | solution.py:77
  187.8 9.6 %while.116 = (s32[]{:T(128)}, f32[4,64,256]{2,1,0:T(8,128)S(1)}, f32[4,256]{1,0:T(4,128)S(1)}, f32[4,256]{1,0:T(4,128)S(1)}, f32[4,256]{1,0:T(4,128)S(1)}, /*ind...) while((s32[]{:T(128)}, f32[4,64,256]{2,1,0:T(8,128)S(1)}, ...), condition=%wide.region_40.41_spmd, body=%wide.region_38.40_spmd.sunk | while | flops 103023616 | bytes 1596609 | solution.py:77
  198.7 10.2 %while.117 = (s32[]{:T(128)}, f32[4,64,256]{2,1,0:T(8,128)S(1)}, f32[4,256]{1,0:T(4,128)S(1)}, f32[4,256]{1,0:T(4,128)S(1)}, f32[4,256]{1,0:T(4,128)S(1)}, /*ind...) while((s32[]{:T(128)}, f32[4,64,256]{2,1,0:T(8,128)S(1)}, ...), condition=%wide.region_45.46_spmd, body=%wide.region_43.45_spmd.sunk | while | flops 103023616 | bytes 1596609 | solution.py:77
  209.5 107.8 %psum.7 = f32[64,64]{0,1:T(8,128)S(1)} all-reduce(f32[64,64]{0,1:T(8,128)S(1)} %convolution_bitcast_fusion.9), channel_id=1, replica_groups=mesh['blk'=64,'grp'=8] {'blk','grp'}, use_global_device_ids=true, to_apply=%region_46.47 | all-reduce | flops 4096 | bytes 32768 | tf_op jit(solution)/shard_map/psum | solution.py:96
  317.3 5.8 %cholesky.16 = f32[64,64]{1,0:T(8,128)S(1)} custom-call(f32[64,64]{1,0:T(8,128)S(1)} %fusion.123), custom_call_target="Cholesky" | custom-call | tf_op jit(solution)/shard_map/jit(cholesky)/cholesky | solution.py:97
  324.5 4.9 %custom-call.6 = f32[1,64,64]{1,2,0:T(8,128)S(1)} custom-call(f32[1,64,64]{2,1,0:T(8,128)S(1)} %get-tuple-element.1067), custom_call_target="InvertDiagBlocksLowerTriangular" | custom-call | tf_op jit(solution)/shard_map/triangular_solve | solution.py:98
  (363 shorter events, 112.6 us)
Async XLA Ops:
  0.6 27.6 %copy-start = (s32[1,256,16]{1,2,0:T(8,128)S(1)}, s32[1,256,16]{1,2,0:T(8,128)}, u32[]{:S(2)}) copy-start(s32[1,256,16]{1,2,0:T(8,128)} %param.26) | copy-start | bytes 49156
  1.6 38.4 %collective-permute-start.2 = (bf16[64,4,256]{2,1,0:T(4,128)(2,1)S(1)}, bf16[64,4,256]{2,1,0:T(4,128)(2,1)S(1)}, u32[]{:S(2)}, u32[]{:S(2)}) collective-permute-start(bf16[64,4,256]{2,1,0:T(4,128)(2,1)S(1)} %reshape_squeeze.6), channel_id=1, source_target_pairs={{504,0},{0,8},{8,16},{16,24},{24,32},{32,40},{40,48},{48,56},{56,6... | collective-permute-start | bytes 393224 | tf_op jit(solution)/shard_map/ppermute | solution.py:17
  6.0 39.2 %collective-permute-start.5 = (bf16[64,4,256]{2,1,0:T(4,128)(2,1)S(1)}, bf16[64,4,256]{2,1,0:T(4,128)(2,1)S(1)}, u32[]{:S(2)}, u32[]{:S(2)}) collective-permute-start(bf16[64,4,256]{2,1,0:T(4,128)(2,1)S(1)} %reshape_squeeze.6), channel_id=1, source_target_pairs={{496,0},{504,8},{0,16},{8,24},{16,32},{24,40},{32,48},{40,56},{48,... | collective-permute-start | bytes 393224 | tf_op jit(solution)/shard_map/ppermute | solution.py:17
  10.9 37.9 %collective-permute-start.8 = (bf16[64,4,256]{2,1,0:T(4,128)(2,1)S(1)}, bf16[64,4,256]{2,1,0:T(4,128)(2,1)S(1)}, u32[]{:S(2)}, u32[]{:S(2)}) collective-permute-start(bf16[64,4,256]{2,1,0:T(4,128)(2,1)S(1)} %reshape_squeeze.6), channel_id=1, source_target_pairs={{488,0},{496,8},{504,16},{0,24},{8,32},{16,40},{24,48},{32,56},{40... | collective-permute-start | bytes 393224 | tf_op jit(solution)/shard_map/ppermute | solution.py:17
  18.4 34.1 %collective-permute-start.11 = (bf16[64,4,256]{2,1,0:T(4,128)(2,1)S(1)}, bf16[64,4,256]{2,1,0:T(4,128)(2,1)S(1)}, u32[]{:S(2)}, u32[]{:S(2)}) collective-permute-start(bf16[64,4,256]{2,1,0:T(4,128)(2,1)S(1)} %reshape_squeeze.6), channel_id=1, source_target_pairs={{480,0},{488,8},{496,16},{504,24},{0,32},{8,40},{16,48},{24,56},{3... | collective-permute-start | bytes 393224 | tf_op jit(solution)/shard_map/ppermute | solution.py:17
  25.4 59.5 %collective-permute-start = (bf16[4,256,128]{2,1,0:T(8,128)(2,1)}, bf16[4,256,128]{2,1,0:T(8,128)(2,1)S(1)}, u32[]{:S(2)}, u32[]{:S(2)}) collective-permute-start(bf16[4,256,128]{2,1,0:T(8,128)(2,1)} %bitcast.90), channel_id=1, source_target_pairs={{504,0},{0,8},{8,16},{16,24},{24,32},{32,40},{40,48},{48,56},{56,6... | collective-permute-start | bytes 786440 | tf_op jit(solution)/shard_map/ppermute | solution.py:17
  28.2 0.7 copy-start.2
  28.3 1.3 copy-start.1
  40.1 28.9 %collective-permute-start.14 = (bf16[64,4,256]{2,1,0:T(4,128)(2,1)S(1)}, bf16[64,4,256]{2,1,0:T(4,128)(2,1)S(1)}, u32[]{:S(2)}, u32[]{:S(2)}) collective-permute-start(bf16[64,4,256]{2,1,0:T(4,128)(2,1)S(1)} %reshape_squeeze.6), channel_id=1, source_target_pairs={{32,0},{40,8},{48,16},{56,24},{64,32},{72,40},{80,48},{88,56},{96,... | collective-permute-start | bytes 393224 | tf_op jit(solution)/shard_map/ppermute | solution.py:17
  45.3 25.9 %collective-permute-start.17 = (bf16[64,4,256]{2,1,0:T(4,128)(2,1)S(1)}, bf16[64,4,256]{2,1,0:T(4,128)(2,1)S(1)}, u32[]{:S(2)}, u32[]{:S(2)}) collective-permute-start(bf16[64,4,256]{2,1,0:T(4,128)(2,1)S(1)} %reshape_squeeze.6), channel_id=1, source_target_pairs={{24,0},{32,8},{40,16},{48,24},{56,32},{64,40},{72,48},{80,56},{88,... | collective-permute-start | bytes 393224 | tf_op jit(solution)/shard_map/ppermute | solution.py:17
  48.9 24.9 %collective-permute-start.20 = (bf16[64,4,256]{2,1,0:T(4,128)(2,1)S(1)}, bf16[64,4,256]{2,1,0:T(4,128)(2,1)S(1)}, u32[]{:S(2)}, u32[]{:S(2)}) collective-permute-start(bf16[64,4,256]{2,1,0:T(4,128)(2,1)S(1)} %reshape_squeeze.6), channel_id=1, source_target_pairs={{16,0},{24,8},{32,16},{40,24},{48,32},{56,40},{64,48},{72,56},{80,... | collective-permute-start | bytes 393224 | tf_op jit(solution)/shard_map/ppermute | solution.py:17
  52.5 26.4 %collective-permute-start.23 = (bf16[64,4,256]{2,1,0:T(4,128)(2,1)S(1)}, bf16[64,4,256]{2,1,0:T(4,128)(2,1)S(1)}, u32[]{:S(2)}, u32[]{:S(2)}) collective-permute-start(bf16[64,4,256]{2,1,0:T(4,128)(2,1)S(1)} %reshape_squeeze.6), channel_id=1, source_target_pairs={{8,0},{16,8},{24,16},{32,24},{40,32},{48,40},{56,48},{64,56},{72,6... | collective-permute-start | bytes 393224 | tf_op jit(solution)/shard_map/ppermute | solution.py:17
  68.9 18.6 %collective-permute-start.1 = (bf16[4,256]{1,0:T(4,128)(2,1)}, bf16[4,256]{1,0:T(4,128)(2,1)S(1)}, u32[]{:S(2)}, u32[]{:S(2)}) collective-permute-start(bf16[4,256]{1,0:T(4,128)(2,1)} %convert_element_type.264), channel_id=1, source_target_pairs={{504,0},{0,8},{8,16},{16,24},{24,32},{32,40},{40,48},{48,56},{56,6... | collective-permute-start | bytes 6152 | tf_op jit(solution)/shard_map/ppermute | solution.py:17
  71.2 33.1 %collective-permute-start.4 = (bf16[4,256]{1,0:T(4,128)(2,1)}, bf16[4,256]{1,0:T(4,128)(2,1)S(1)}, u32[]{:S(2)}, u32[]{:S(2)}) collective-permute-start(bf16[4,256]{1,0:T(4,128)(2,1)} %convert_element_type.264), channel_id=1, source_target_pairs={{496,0},{504,8},{0,16},{8,24},{16,32},{24,40},{32,48},{40,56},{48,... | collective-permute-start | bytes 6152 | tf_op jit(solution)/shard_map/ppermute | solution.py:17
  73.7 25.4 %collective-permute-start.3 = (bf16[4,256,128]{2,1,0:T(8,128)(2,1)}, bf16[4,256,128]{2,1,0:T(8,128)(2,1)S(1)}, u32[]{:S(2)}, u32[]{:S(2)}) collective-permute-start(bf16[4,256,128]{2,1,0:T(8,128)(2,1)} %bitcast.90), channel_id=1, source_target_pairs={{496,0},{504,8},{0,16},{8,24},{16,32},{24,40},{32,48},{40,56},{48,... | collective-permute-start | bytes 786440 | tf_op jit(solution)/shard_map/ppermute | solution.py:17
  79.0 48.9 %collective-permute-start.7 = (bf16[4,256]{1,0:T(4,128)(2,1)}, bf16[4,256]{1,0:T(4,128)(2,1)S(1)}, u32[]{:S(2)}, u32[]{:S(2)}) collective-permute-start(bf16[4,256]{1,0:T(4,128)(2,1)} %convert_element_type.264), channel_id=1, source_target_pairs={{488,0},{496,8},{504,16},{0,24},{8,32},{16,40},{24,48},{32,56},{40... | collective-permute-start | bytes 6152 | tf_op jit(solution)/shard_map/ppermute | solution.py:17
  85.0 35.4 %collective-permute-start.6 = (bf16[4,256,128]{2,1,0:T(8,128)(2,1)}, bf16[4,256,128]{2,1,0:T(8,128)(2,1)S(1)}, u32[]{:S(2)}, u32[]{:S(2)}) collective-permute-start(bf16[4,256,128]{2,1,0:T(8,128)(2,1)} %bitcast.90), channel_id=1, source_target_pairs={{488,0},{496,8},{504,16},{0,24},{8,32},{16,40},{24,48},{32,56},{40... | collective-permute-start | bytes 786440 | tf_op jit(solution)/shard_map/ppermute | solution.py:17
  87.6 58.5 %collective-permute-start.10 = (bf16[4,256]{1,0:T(4,128)(2,1)}, bf16[4,256]{1,0:T(4,128)(2,1)S(1)}, u32[]{:S(2)}, u32[]{:S(2)}) collective-permute-start(bf16[4,256]{1,0:T(4,128)(2,1)} %convert_element_type.264), channel_id=1, source_target_pairs={{480,0},{488,8},{496,16},{504,24},{0,32},{8,40},{16,48},{24,56},{3... | collective-permute-start | bytes 6152 | tf_op jit(solution)/shard_map/ppermute | solution.py:17
  99.2 44.3 %collective-permute-start.9 = (bf16[4,256,128]{2,1,0:T(8,128)(2,1)}, bf16[4,256,128]{2,1,0:T(8,128)(2,1)S(1)}, u32[]{:S(2)}, u32[]{:S(2)}) collective-permute-start(bf16[4,256,128]{2,1,0:T(8,128)(2,1)} %bitcast.90), channel_id=1, source_target_pairs={{480,0},{488,8},{496,16},{504,24},{0,32},{8,40},{16,48},{24,56},{3... | collective-permute-start | bytes 786440 | tf_op jit(solution)/shard_map/ppermute | solution.py:17
  104.3 58.5 %collective-permute-start.13 = (bf16[4,256]{1,0:T(4,128)(2,1)}, bf16[4,256]{1,0:T(4,128)(2,1)S(1)}, u32[]{:S(2)}, u32[]{:S(2)}) collective-permute-start(bf16[4,256]{1,0:T(4,128)(2,1)} %convert_element_type.264), channel_id=1, source_target_pairs={{32,0},{40,8},{48,16},{56,24},{64,32},{72,40},{80,48},{88,56},{96,... | collective-permute-start | bytes 6152 | tf_op jit(solution)/shard_map/ppermute | solution.py:17
  120.4 37.3 %collective-permute-start.12 = (bf16[4,256,128]{2,1,0:T(8,128)(2,1)}, bf16[4,256,128]{2,1,0:T(8,128)(2,1)S(1)}, u32[]{:S(2)}, u32[]{:S(2)}) collective-permute-start(bf16[4,256,128]{2,1,0:T(8,128)(2,1)} %bitcast.90), channel_id=1, source_target_pairs={{32,0},{40,8},{48,16},{56,24},{64,32},{72,40},{80,48},{88,56},{96,... | collective-permute-start | bytes 786440 | tf_op jit(solution)/shard_map/ppermute | solution.py:17
  127.9 49.9 %collective-permute-start.16 = (bf16[4,256]{1,0:T(4,128)(2,1)}, bf16[4,256]{1,0:T(4,128)(2,1)S(1)}, u32[]{:S(2)}, u32[]{:S(2)}) collective-permute-start(bf16[4,256]{1,0:T(4,128)(2,1)} %convert_element_type.264), channel_id=1, source_target_pairs={{24,0},{32,8},{40,16},{48,24},{56,32},{64,40},{72,48},{80,56},{88,... | collective-permute-start | bytes 6152 | tf_op jit(solution)/shard_map/ppermute | solution.py:17
  143.5 32.0 %collective-permute-start.15 = (bf16[4,256,128]{2,1,0:T(8,128)(2,1)}, bf16[4,256,128]{2,1,0:T(8,128)(2,1)S(1)}, u32[]{:S(2)}, u32[]{:S(2)}) collective-permute-start(bf16[4,256,128]{2,1,0:T(8,128)(2,1)} %bitcast.90), channel_id=1, source_target_pairs={{24,0},{32,8},{40,16},{48,24},{56,32},{64,40},{72,48},{80,56},{88,... | collective-permute-start | bytes 786440 | tf_op jit(solution)/shard_map/ppermute | solution.py:17
  146.1 41.7 %collective-permute-start.19 = (bf16[4,256]{1,0:T(4,128)(2,1)}, bf16[4,256]{1,0:T(4,128)(2,1)S(1)}, u32[]{:S(2)}, u32[]{:S(2)}) collective-permute-start(bf16[4,256]{1,0:T(4,128)(2,1)} %convert_element_type.264), channel_id=1, source_target_pairs={{16,0},{24,8},{32,16},{40,24},{48,32},{56,40},{64,48},{72,56},{80,... | collective-permute-start | bytes 6152 | tf_op jit(solution)/shard_map/ppermute | solution.py:17
  157.7 29.8 %collective-permute-start.18 = (bf16[4,256,128]{2,1,0:T(8,128)(2,1)}, bf16[4,256,128]{2,1,0:T(8,128)(2,1)S(1)}, u32[]{:S(2)}, u32[]{:S(2)}) collective-permute-start(bf16[4,256,128]{2,1,0:T(8,128)(2,1)} %bitcast.90), channel_id=1, source_target_pairs={{16,0},{24,8},{32,16},{40,24},{48,32},{56,40},{64,48},{72,56},{80,... | collective-permute-start | bytes 786440 | tf_op jit(solution)/shard_map/ppermute | solution.py:17
  162.8 35.9 %collective-permute-start.22 = (bf16[4,256]{1,0:T(4,128)(2,1)}, bf16[4,256]{1,0:T(4,128)(2,1)S(1)}, u32[]{:S(2)}, u32[]{:S(2)}) collective-permute-start(bf16[4,256]{1,0:T(4,128)(2,1)} %convert_element_type.264), channel_id=1, source_target_pairs={{8,0},{16,8},{24,16},{32,24},{40,32},{48,40},{56,48},{64,56},{72,6... | collective-permute-start | bytes 6152 | tf_op jit(solution)/shard_map/ppermute | solution.py:17
  175.5 21.9 %collective-permute-start.21 = (bf16[4,256,128]{2,1,0:T(8,128)(2,1)}, bf16[4,256,128]{2,1,0:T(8,128)(2,1)}, u32[]{:S(2)}, u32[]{:S(2)}) collective-permute-start(bf16[4,256,128]{2,1,0:T(8,128)(2,1)} %bitcast.90), channel_id=1, source_target_pairs={{8,0},{16,8},{24,16},{32,24},{40,32},{48,40},{56,48},{64,56},{72,6... | collective-permute-start | bytes 786440 | tf_op jit(solution)/shard_map/ppermute | solution.py:17
where the time goes:
time: 335 us; the launch traced here: 331 us
  blocking collectives  108 us (32%)
  starting transfers between devices  101 us (30%)
  matrix products  60.8 us (18%)
  other arithmetic  45.7 us (14%)
  local copies, waits for them, and re-layouts  12.9 us (4%)
    psum x1, blocking collectives, local(): gram_matrix = lax.psum(gram_local, ('blk', 'grp'))  108 us
    ppermute x24, starting transfers between devices, passed_along(): return lax.ppermute(block, axis, route)  101 us
    dot_general x36, matrix products, tile_terms(): jnp.einsum('pe,cqe->cpq', row_points, col_points, preferred_element_type=...  51.8 us
    convert_element_type x36, other arithmetic, tile_terms(): row_scales.astype(jnp.float32)[None, :, None]  24.9 us
    dot_general x36, matrix products, tile_terms(): jnp.einsum('cpq,kcq->kp', weights, col_panel, preferred_element_type=jnp....  7.53 us
    gather x1, local copies, waits for them, and re-layouts, local(): partner = jnp.take_along_axis(own_points, partner_pos[:, :, None], axis=1)  6.76 us
  transfers between devices with their start and end apart: 24, of which 0 were waited for; matrix products, arithmetic and copies ran while one was open for 28% of the time, Pallas kernels for 0%

commit v1 on v0

--- a/solution.py
+++ b/solution.py
@@ -93,7 +93,8 @@
     gram_local = jnp.dot(
         walked, walked.T, precision=lax.Precision.HIGHEST, preferred_element_type=jnp.float32
     )
-    gram_matrix = lax.psum(gram_local, ("blk", "grp"))
+    parts = lax.all_gather(gram_local, ("blk", "grp"))
+    gram_matrix = jnp.sum(parts, axis=0)
     lower_factor = jnp.linalg.cholesky(gram_matrix)
     solved = lax.linalg.triangular_solve(lower_factor, walked, left_side=True, lower=True)
     point_total = points.shape[1] * lax.axis_size("blk") * lax.axis_size("grp")

time: 335 us -> 472 us (1.41)
  waiting for transfers between devices: 0.06 us -> 222 us
  blocking collectives: 108 us -> 0 us
  between operations: 1.63 us -> 15 us
  other arithmetic: 45.7 us -> 54.1 us
    all_gather x0 -> x1, waiting for transfers between devices: none -> 222 us  [local(): parts = lax.all_gather(gram_local, ('blk', 'grp'))]
    psum x1 -> x0, blocking collectives: 108 us -> none  [local(): gram_matrix = lax.psum(gram_local, ('blk', 'grp'))]
    reduce_sum x0 -> x1, other arithmetic: none -> 6.94 us  [local(): gram_matrix = jnp.sum(parts, axis=0)]
  transfers between devices with their start and end apart: 24 -> 25, of which waited for: 0 -> 1; matrix products, arithmetic and copies ran while one was open for 28% -> 20% of each run, Pallas kernels for 0% -> 0%
where the time goes in v1:
time: 472 us; the launch traced here: 468 us
  waiting for transfers between devices  222 us (47%)
  starting transfers between devices  101 us (21%)
  matrix products  61.6 us (13%)
  other arithmetic  54.1 us (11%)
  between operations  15 us (3%)
  local copies, waits for them, and re-layouts  13 us (3%)
    all_gather x1, waiting for transfers between devices, local(): parts = lax.all_gather(gram_local, ('blk', 'grp'))  222 us
    ppermute x24, starting transfers between devices, passed_along(): return lax.ppermute(block, axis, route)  101 us
    dot_general x36, matrix products, tile_terms(): jnp.einsum('pe,cqe->cpq', row_points, col_points, preferred_element_type=...  51.9 us
    convert_element_type x36, other arithmetic, tile_terms(): row_scales.astype(jnp.float32)[None, :, None]  24.9 us
  transfers between devices with their start and end apart: 25, of which 1 were waited for; matrix products, arithmetic and copies ran while one was open for 20% of the time, Pallas kernels for 0%

profile of v1, /device:TPU:1, one launch (start us, length us, event | category | flops | bytes accessed | tf_op | source)
XLA Modules:
  0.0 468.3 jit_solution(8715827963982613735)
XLA Ops:
  8.2 4.4 collective-permute-start.2
  12.6 4.9 %collective-permute-start.5 = (bf16[64,4,256]{2,1,0:T(4,128)(2,1)S(1)}, bf16[64,4,256]{2,1,0:T(4,128)(2,1)S(1)}, u32[]{:S(2)}, u32[]{:S(2)}) collective-permute-start(bf16[64,4,256]{2,1,0:T(4,128)(2,1)S(1)} %reshape_squeeze.6), channel_id=1, source_target_pairs={{496,0},{504,8},{0,16},{8,24},{16,32},{24,40},{32,48},{40,56},{48,... | collective-permute-start | bytes 393224 | tf_op jit(solution)/shard_map/ppermute | solution.py:17
  17.5 7.5 %collective-permute-start.8 = (bf16[64,4,256]{2,1,0:T(4,128)(2,1)S(1)}, bf16[64,4,256]{2,1,0:T(4,128)(2,1)S(1)}, u32[]{:S(2)}, u32[]{:S(2)}) collective-permute-start(bf16[64,4,256]{2,1,0:T(4,128)(2,1)S(1)} %reshape_squeeze.6), channel_id=1, source_target_pairs={{488,0},{496,8},{504,16},{0,24},{8,32},{16,40},{24,48},{32,56},{40... | collective-permute-start | bytes 393224 | tf_op jit(solution)/shard_map/ppermute | solution.py:17
  25.0 7.0 %collective-permute-start.11 = (bf16[64,4,256]{2,1,0:T(4,128)(2,1)S(1)}, bf16[64,4,256]{2,1,0:T(4,128)(2,1)S(1)}, u32[]{:S(2)}, u32[]{:S(2)}) collective-permute-start(bf16[64,4,256]{2,1,0:T(4,128)(2,1)S(1)} %reshape_squeeze.6), channel_id=1, source_target_pairs={{480,0},{488,8},{496,16},{504,24},{0,32},{8,40},{16,48},{24,56},{3... | collective-permute-start | bytes 393224 | tf_op jit(solution)/shard_map/ppermute | solution.py:17
  32.0 2.6 collective-permute-start
  37.6 6.8 %gather_fusion = bf16[1024,128]{1,0:T(8,128)(2,1)S(1)} fusion(bf16[4,256,128]{2,1,0:T(8,128)(2,1)} %bitcast.507, s32[1024]{0:T(1024)S(1)} %bitcast.505), kind=kCustom, calls=%fused_computation | custom fusion | bytes 532480 | tf_op jit(solution)/shard_map/jit(take_along_axis)/gather | solution.py:46
  48.1 5.2 %collective-permute-start.14 = (bf16[64,4,256]{2,1,0:T(4,128)(2,1)S(1)}, bf16[64,4,256]{2,1,0:T(4,128)(2,1)S(1)}, u32[]{:S(2)}, u32[]{:S(2)}) collective-permute-start(bf16[64,4,256]{2,1,0:T(4,128)(2,1)S(1)} %reshape_squeeze.6), channel_id=1, source_target_pairs={{32,0},{40,8},{48,16},{56,24},{64,32},{72,40},{80,48},{88,56},{96,... | collective-permute-start | bytes 393224 | tf_op jit(solution)/shard_map/ppermute | solution.py:17
  53.3 3.6 collective-permute-start.17
  56.9 3.7 collective-permute-start.20
  60.6 3.1 collective-permute-start.23
  63.7 13.1 %while.109 = (s32[]{:T(128)}, f32[4,64,256]{2,1,0:T(8,128)S(1)}, f32[4,256]{1,0:T(4,128)S(1)}, f32[4,256]{1,0:T(4,128)S(1)}, bf16[4,256,128]{2,1,0:T(8,128)(2,1)...) while((s32[]{:T(128)}, f32[4,64,256]{2,1,0:T(8,128)S(1)}, ...), condition=%wide.region_5.6_spmd, body=%wide.region_3.0_spmd.sunk | while | flops 103023616 | bytes 1596585 | solution.py:77
  79.2 2.5 collective-permute-start.4
  81.8 5.2 %collective-permute-start.3 = (bf16[4,256,128]{2,1,0:T(8,128)(2,1)}, bf16[4,256,128]{2,1,0:T(8,128)(2,1)S(1)}, u32[]{:S(2)}, u32[]{:S(2)}) collective-permute-start(bf16[4,256,128]{2,1,0:T(8,128)(2,1)} %get-tuple-element.2157), channel_id=1, source_target_pairs={{496,0},{504,8},{0,16},{8,24},{16,32},{24,40},{32,48},{40,56},{48,... | collective-permute-start | bytes 786440 | tf_op jit(solution)/shard_map/ppermute | solution.py:17
  87.0 5.9 %collective-permute-start.7 = (bf16[4,256]{1,0:T(4,128)(2,1)}, bf16[4,256]{1,0:T(4,128)(2,1)S(1)}, u32[]{:S(2)}, u32[]{:S(2)}) collective-permute-start(bf16[4,256]{1,0:T(4,128)(2,1)} %convert_element_type.264), channel_id=1, source_target_pairs={{488,0},{496,8},{504,16},{0,24},{8,32},{16,40},{24,48},{32,56},{40... | collective-permute-start | bytes 6152 | tf_op jit(solution)/shard_map/ppermute | solution.py:17
  97.6 9.6 %while.110 = (s32[]{:T(128)}, f32[4,64,256]{2,1,0:T(8,128)S(1)}, f32[4,256]{1,0:T(4,128)S(1)}, f32[4,256]{1,0:T(4,128)S(1)}, f32[4,256]{1,0:T(4,128)S(1)}, /*ind...) while((s32[]{:T(128)}, f32[4,64,256]{2,1,0:T(8,128)S(1)}, ...), condition=%wide.region_10.11_spmd, body=%wide.region_8.10_spmd.sunk | while | flops 103023616 | bytes 1596609 | solution.py:77
  107.2 4.9 %collective-permute-start.9 = (bf16[4,256,128]{2,1,0:T(8,128)(2,1)}, bf16[4,256,128]{2,1,0:T(8,128)(2,1)S(1)}, u32[]{:S(2)}, u32[]{:S(2)}) collective-permute-start(bf16[4,256,128]{2,1,0:T(8,128)(2,1)} %get-tuple-element.2160), channel_id=1, source_target_pairs={{480,0},{488,8},{496,16},{504,24},{0,32},{8,40},{16,48},{24,56},{3... | collective-permute-start | bytes 786440 | tf_op jit(solution)/shard_map/ppermute | solution.py:17
  112.3 6.4 %collective-permute-start.13 = (bf16[4,256]{1,0:T(4,128)(2,1)}, bf16[4,256]{1,0:T(4,128)(2,1)S(1)}, u32[]{:S(2)}, u32[]{:S(2)}) collective-permute-start(bf16[4,256]{1,0:T(4,128)(2,1)} %convert_element_type.264), channel_id=1, source_target_pairs={{32,0},{40,8},{48,16},{56,24},{64,32},{72,40},{80,48},{88,56},{96,... | collective-permute-start | bytes 6152 | tf_op jit(solution)/shard_map/ppermute | solution.py:17
  118.8 9.6 %while.111 = (s32[]{:T(128)}, f32[4,64,256]{2,1,0:T(8,128)S(1)}, f32[4,256]{1,0:T(4,128)S(1)}, f32[4,256]{1,0:T(4,128)S(1)}, f32[4,256]{1,0:T(4,128)S(1)}, /*ind...) while((s32[]{:T(128)}, f32[4,64,256]{2,1,0:T(8,128)S(1)}, ...), condition=%wide.region_15.16_spmd, body=%wide.region_13.15_spmd.sunk | while | flops 103023616 | bytes 1596609 | solution.py:77
  128.4 7.3 %collective-permute-start.12 = (bf16[4,256,128]{2,1,0:T(8,128)(2,1)}, bf16[4,256,128]{2,1,0:T(8,128)(2,1)S(1)}, u32[]{:S(2)}, u32[]{:S(2)}) collective-permute-start(bf16[4,256,128]{2,1,0:T(8,128)(2,1)} %get-tuple-element.2162), channel_id=1, source_target_pairs={{32,0},{40,8},{48,16},{56,24},{64,32},{72,40},{80,48},{88,56},{96,... | collective-permute-start | bytes 786440 | tf_op jit(solution)/shard_map/ppermute | solution.py:17
  135.9 5.9 %collective-permute-start.16 = (bf16[4,256]{1,0:T(4,128)(2,1)}, bf16[4,256]{1,0:T(4,128)(2,1)S(1)}, u32[]{:S(2)}, u32[]{:S(2)}) collective-permute-start(bf16[4,256]{1,0:T(4,128)(2,1)} %convert_element_type.264), channel_id=1, source_target_pairs={{24,0},{32,8},{40,16},{48,24},{56,32},{64,40},{72,48},{80,56},{88,... | collective-permute-start | bytes 6152 | tf_op jit(solution)/shard_map/ppermute | solution.py:17
  141.9 9.6 %while.112 = (s32[]{:T(128)}, f32[4,64,256]{2,1,0:T(8,128)S(1)}, f32[4,256]{1,0:T(4,128)S(1)}, f32[4,256]{1,0:T(4,128)S(1)}, f32[4,256]{1,0:T(4,128)S(1)}, /*ind...) while((s32[]{:T(128)}, f32[4,64,256]{2,1,0:T(8,128)S(1)}, ...), condition=%wide.region_20.21_spmd, body=%wide.region_18.20_spmd.sunk | while | flops 103023616 | bytes 1596609 | solution.py:77
  156.1 9.6 %while.113 = (s32[]{:T(128)}, f32[4,64,256]{2,1,0:T(8,128)S(1)}, f32[4,256]{1,0:T(4,128)S(1)}, f32[4,256]{1,0:T(4,128)S(1)}, f32[4,256]{1,0:T(4,128)S(1)}, /*ind...) while((s32[]{:T(128)}, f32[4,64,256]{2,1,0:T(8,128)S(1)}, ...), condition=%wide.region_25.26_spmd, body=%wide.region_23.25_spmd.sunk | while | flops 103023616 | bytes 1596609 | solution.py:77
  165.8 4.8 %collective-permute-start.18 = (bf16[4,256,128]{2,1,0:T(8,128)(2,1)}, bf16[4,256,128]{2,1,0:T(8,128)(2,1)S(1)}, u32[]{:S(2)}, u32[]{:S(2)}) collective-permute-start(bf16[4,256,128]{2,1,0:T(8,128)(2,1)} %get-tuple-element.2166), channel_id=1, source_target_pairs={{16,0},{24,8},{32,16},{40,24},{48,32},{56,40},{64,48},{72,56},{80,... | collective-permute-start | bytes 786440 | tf_op jit(solution)/shard_map/ppermute | solution.py:17
  170.8 3.1 collective-permute-start.22
  174.0 9.6 %while.114 = (s32[]{:T(128)}, f32[4,64,256]{2,1,0:T(8,128)S(1)}, f32[4,256]{1,0:T(4,128)S(1)}, f32[4,256]{1,0:T(4,128)S(1)}, f32[4,256]{1,0:T(4,128)S(1)}, /*ind...) while((s32[]{:T(128)}, f32[4,64,256]{2,1,0:T(8,128)S(1)}, ...), condition=%wide.region_30.31_spmd, body=%wide.region_28.30_spmd.sunk | while | flops 103023616 | bytes 1596609 | solution.py:77
  186.0 9.6 %while.115 = (s32[]{:T(128)}, f32[4,64,256]{2,1,0:T(8,128)S(1)}, f32[4,256]{1,0:T(4,128)S(1)}, f32[4,256]{1,0:T(4,128)S(1)}, f32[4,256]{1,0:T(4,128)S(1)}, /*ind...) while((s32[]{:T(128)}, f32[4,64,256]{2,1,0:T(8,128)S(1)}, ...), condition=%wide.region_35.36_spmd, body=%wide.region_33.35_spmd.sunk | while | flops 103023616 | bytes 1596609 | solution.py:77
  195.9 9.6 %while.116 = (s32[]{:T(128)}, f32[4,64,256]{2,1,0:T(8,128)S(1)}, f32[4,256]{1,0:T(4,128)S(1)}, f32[4,256]{1,0:T(4,128)S(1)}, f32[4,256]{1,0:T(4,128)S(1)}, /*ind...) while((s32[]{:T(128)}, f32[4,64,256]{2,1,0:T(8,128)S(1)}, ...), condition=%wide.region_40.41_spmd, body=%wide.region_38.40_spmd.sunk | while | flops 103023616 | bytes 1596609 | solution.py:77
  206.8 10.2 %while.117 = (s32[]{:T(128)}, f32[4,64,256]{2,1,0:T(8,128)S(1)}, f32[4,256]{1,0:T(4,128)S(1)}, f32[4,256]{1,0:T(4,128)S(1)}, f32[4,256]{1,0:T(4,128)S(1)}, /*ind...) while((s32[]{:T(128)}, f32[4,64,256]{2,1,0:T(8,128)S(1)}, ...), condition=%wide.region_45.46_spmd, body=%wide.region_43.45_spmd.sunk | while | flops 103023616 | bytes 1596609 | solution.py:77
  218.2 222.3 %all-gather.3.cloned.1.call-done = f32[32768,64]{1,0:T(8,128)} async-done(((f32[64,64]{1,0:T(8,128)}), f32[32768,64]{1,0:T(8,128)}) %all-gather.3.cloned.1.call-update) | async-done | bytes 8388624 | tf_op jit(solution)/shard_map/all_gather | solution.py:96
  440.5 6.9 %reduce_sum.198 = f32[64,64]{1,0:T(8,128)S(1)} reduce(f32[512,64,64]{2,1,0:T(8,128)} %bitcast.509, f32[]{:T(128)} %constant.264.clone.1), dimensions={0}, to_apply=%region_46.47 | reduce | flops 2093056 | bytes 8404996 | tf_op jit(solution)/shard_map/reduce_sum | solution.py:97
  447.5 5.8 %cholesky.16 = f32[64,64]{1,0:T(8,128)S(1)} custom-call(f32[64,64]{1,0:T(8,128)S(1)} %fusion.123), custom_call_target="Cholesky" | custom-call | tf_op jit(solution)/shard_map/jit(cholesky)/cholesky | solution.py:98
  454.7 4.9 %custom-call.6 = f32[1,64,64]{1,2,0:T(8,128)S(1)} custom-call(f32[1,64,64]{2,1,0:T(8,128)S(1)} %get-tuple-element.1165), custom_call_target="InvertDiagBlocksLowerTriangular" | custom-call | tf_op jit(solution)/shard_map/triangular_solve | solution.py:99
  (362 shorter events, 117.2 us)
Async XLA Ops:
  7.2 27.6 %copy-start = (s32[1,256,16]{1,2,0:T(8,128)S(1)}, s32[1,256,16]{1,2,0:T(8,128)}, u32[]{:S(2)}) copy-start(s32[1,256,16]{1,2,0:T(8,128)} %param.26) | copy-start | bytes 49156
  7.2 433.3 %all-gather.3.cloned.1.call-start = ((), (), s32[]{:S(2)}) async-start(), calls=%async_computation | async-start | bytes 16809984 | tf_op jit(solution)/shard_map/all_gather | solution.py:96
  8.2 39.9 %collective-permute-start.2 = (bf16[64,4,256]{2,1,0:T(4,128)(2,1)S(1)}, bf16[64,4,256]{2,1,0:T(4,128)(2,1)S(1)}, u32[]{:S(2)}, u32[]{:S(2)}) collective-permute-start(bf16[64,4,256]{2,1,0:T(4,128)(2,1)S(1)} %reshape_squeeze.6), channel_id=1, source_target_pairs={{504,0},{0,8},{8,16},{16,24},{24,32},{32,40},{40,48},{48,56},{56,6... | collective-permute-start | bytes 393224 | tf_op jit(solution)/shard_map/ppermute | solution.py:17
  12.6 40.7 %collective-permute-start.5 = (bf16[64,4,256]{2,1,0:T(4,128)(2,1)S(1)}, bf16[64,4,256]{2,1,0:T(4,128)(2,1)S(1)}, u32[]{:S(2)}, u32[]{:S(2)}) collective-permute-start(bf16[64,4,256]{2,1,0:T(4,128)(2,1)S(1)} %reshape_squeeze.6), channel_id=1, source_target_pairs={{496,0},{504,8},{0,16},{8,24},{16,32},{24,40},{32,48},{40,56},{48,... | collective-permute-start | bytes 393224 | tf_op jit(solution)/shard_map/ppermute | solution.py:17
  17.5 39.4 %collective-permute-start.8 = (bf16[64,4,256]{2,1,0:T(4,128)(2,1)S(1)}, bf16[64,4,256]{2,1,0:T(4,128)(2,1)S(1)}, u32[]{:S(2)}, u32[]{:S(2)}) collective-permute-start(bf16[64,4,256]{2,1,0:T(4,128)(2,1)S(1)} %reshape_squeeze.6), channel_id=1, source_target_pairs={{488,0},{496,8},{504,16},{0,24},{8,32},{16,40},{24,48},{32,56},{40... | collective-permute-start | bytes 393224 | tf_op jit(solution)/shard_map/ppermute | solution.py:17
  25.0 35.6 %collective-permute-start.11 = (bf16[64,4,256]{2,1,0:T(4,128)(2,1)S(1)}, bf16[64,4,256]{2,1,0:T(4,128)(2,1)S(1)}, u32[]{:S(2)}, u32[]{:S(2)}) collective-permute-start(bf16[64,4,256]{2,1,0:T(4,128)(2,1)S(1)} %reshape_squeeze.6), channel_id=1, source_target_pairs={{480,0},{488,8},{496,16},{504,24},{0,32},{8,40},{16,48},{24,56},{3... | collective-permute-start | bytes 393224 | tf_op jit(solution)/shard_map/ppermute | solution.py:17
  32.0 61.0 %collective-permute-start = (bf16[4,256,128]{2,1,0:T(8,128)(2,1)}, bf16[4,256,128]{2,1,0:T(8,128)(2,1)S(1)}, u32[]{:S(2)}, u32[]{:S(2)}) collective-permute-start(bf16[4,256,128]{2,1,0:T(8,128)(2,1)} %bitcast.506), channel_id=1, source_target_pairs={{504,0},{0,8},{8,16},{16,24},{24,32},{32,40},{40,48},{48,56},{56,6... | collective-permute-start | bytes 786440 | tf_op jit(solution)/shard_map/ppermute | solution.py:17
  48.1 28.9 %collective-permute-start.14 = (bf16[64,4,256]{2,1,0:T(4,128)(2,1)S(1)}, bf16[64,4,256]{2,1,0:T(4,128)(2,1)S(1)}, u32[]{:S(2)}, u32[]{:S(2)}) collective-permute-start(bf16[64,4,256]{2,1,0:T(4,128)(2,1)S(1)} %reshape_squeeze.6), channel_id=1, source_target_pairs={{32,0},{40,8},{48,16},{56,24},{64,32},{72,40},{80,48},{88,56},{96,... | collective-permute-start | bytes 393224 | tf_op jit(solution)/shard_map/ppermute | solution.py:17
  53.3 25.9 %collective-permute-start.17 = (bf16[64,4,256]{2,1,0:T(4,128)(2,1)S(1)}, bf16[64,4,256]{2,1,0:T(4,128)(2,1)S(1)}, u32[]{:S(2)}, u32[]{:S(2)}) collective-permute-start(bf16[64,4,256]{2,1,0:T(4,128)(2,1)S(1)} %reshape_squeeze.6), channel_id=1, source_target_pairs={{24,0},{32,8},{40,16},{48,24},{56,32},{64,40},{72,48},{80,56},{88,... | collective-permute-start | bytes 393224 | tf_op jit(solution)/shard_map/ppermute | solution.py:17
  56.9 24.9 %collective-permute-start.20 = (bf16[64,4,256]{2,1,0:T(4,128)(2,1)S(1)}, bf16[64,4,256]{2,1,0:T(4,128)(2,1)S(1)}, u32[]{:S(2)}, u32[]{:S(2)}) collective-permute-start(bf16[64,4,256]{2,1,0:T(4,128)(2,1)S(1)} %reshape_squeeze.6), channel_id=1, source_target_pairs={{16,0},{24,8},{32,16},{40,24},{48,32},{56,40},{64,48},{72,56},{80,... | collective-permute-start | bytes 393224 | tf_op jit(solution)/shard_map/ppermute | solution.py:17
  60.6 26.5 %collective-permute-start.23 = (bf16[64,4,256]{2,1,0:T(4,128)(2,1)S(1)}, bf16[64,4,256]{2,1,0:T(4,128)(2,1)S(1)}, u32[]{:S(2)}, u32[]{:S(2)}) collective-permute-start(bf16[64,4,256]{2,1,0:T(4,128)(2,1)S(1)} %reshape_squeeze.6), channel_id=1, source_target_pairs={{8,0},{16,8},{24,16},{32,24},{40,32},{48,40},{56,48},{64,56},{72,6... | collective-permute-start | bytes 393224 | tf_op jit(solution)/shard_map/ppermute | solution.py:17
  77.0 18.6 %collective-permute-start.1 = (bf16[4,256]{1,0:T(4,128)(2,1)}, bf16[4,256]{1,0:T(4,128)(2,1)S(1)}, u32[]{:S(2)}, u32[]{:S(2)}) collective-permute-start(bf16[4,256]{1,0:T(4,128)(2,1)} %convert_element_type.264), channel_id=1, source_target_pairs={{504,0},{0,8},{8,16},{16,24},{24,32},{32,40},{40,48},{48,56},{56,6... | collective-permute-start | bytes 6152 | tf_op jit(solution)/shard_map/ppermute | solution.py:17
  79.2 33.1 %collective-permute-start.4 = (bf16[4,256]{1,0:T(4,128)(2,1)}, bf16[4,256]{1,0:T(4,128)(2,1)S(1)}, u32[]{:S(2)}, u32[]{:S(2)}) collective-permute-start(bf16[4,256]{1,0:T(4,128)(2,1)} %convert_element_type.264), channel_id=1, source_target_pairs={{496,0},{504,8},{0,16},{8,24},{16,32},{24,40},{32,48},{40,56},{48,... | collective-permute-start | bytes 6152 | tf_op jit(solution)/shard_map/ppermute | solution.py:17
  81.8 25.4 %collective-permute-start.3 = (bf16[4,256,128]{2,1,0:T(8,128)(2,1)}, bf16[4,256,128]{2,1,0:T(8,128)(2,1)S(1)}, u32[]{:S(2)}, u32[]{:S(2)}) collective-permute-start(bf16[4,256,128]{2,1,0:T(8,128)(2,1)} %get-tuple-element.2157), channel_id=1, source_target_pairs={{496,0},{504,8},{0,16},{8,24},{16,32},{24,40},{32,48},{40,56},{48,... | collective-permute-start | bytes 786440 | tf_op jit(solution)/shard_map/ppermute | solution.py:17
  87.0 48.9 %collective-permute-start.7 = (bf16[4,256]{1,0:T(4,128)(2,1)}, bf16[4,256]{1,0:T(4,128)(2,1)S(1)}, u32[]{:S(2)}, u32[]{:S(2)}) collective-permute-start(bf16[4,256]{1,0:T(4,128)(2,1)} %convert_element_type.264), channel_id=1, source_target_pairs={{488,0},{496,8},{504,16},{0,24},{8,32},{16,40},{24,48},{32,56},{40... | collective-permute-start | bytes 6152 | tf_op jit(solution)/shard_map/ppermute | solution.py:17
  93.0 35.5 %collective-permute-start.6 = (bf16[4,256,128]{2,1,0:T(8,128)(2,1)}, bf16[4,256,128]{2,1,0:T(8,128)(2,1)S(1)}, u32[]{:S(2)}, u32[]{:S(2)}) collective-permute-start(bf16[4,256,128]{2,1,0:T(8,128)(2,1)} %get-tuple-element.2157), channel_id=1, source_target_pairs={{488,0},{496,8},{504,16},{0,24},{8,32},{16,40},{24,48},{32,56},{40... | collective-permute-start | bytes 786440 | tf_op jit(solution)/shard_map/ppermute | solution.py:17
  95.6 58.6 %collective-permute-start.10 = (bf16[4,256]{1,0:T(4,128)(2,1)}, bf16[4,256]{1,0:T(4,128)(2,1)S(1)}, u32[]{:S(2)}, u32[]{:S(2)}) collective-permute-start(bf16[4,256]{1,0:T(4,128)(2,1)} %convert_element_type.264), channel_id=1, source_target_pairs={{480,0},{488,8},{496,16},{504,24},{0,32},{8,40},{16,48},{24,56},{3... | collective-permute-start | bytes 6152 | tf_op jit(solution)/shard_map/ppermute | solution.py:17
  107.2 44.3 %collective-permute-start.9 = (bf16[4,256,128]{2,1,0:T(8,128)(2,1)}, bf16[4,256,128]{2,1,0:T(8,128)(2,1)S(1)}, u32[]{:S(2)}, u32[]{:S(2)}) collective-permute-start(bf16[4,256,128]{2,1,0:T(8,128)(2,1)} %get-tuple-element.2160), channel_id=1, source_target_pairs={{480,0},{488,8},{496,16},{504,24},{0,32},{8,40},{16,48},{24,56},{3... | collective-permute-start | bytes 786440 | tf_op jit(solution)/shard_map/ppermute | solution.py:17
  112.3 58.5 %collective-permute-start.13 = (bf16[4,256]{1,0:T(4,128)(2,1)}, bf16[4,256]{1,0:T(4,128)(2,1)S(1)}, u32[]{:S(2)}, u32[]{:S(2)}) collective-permute-start(bf16[4,256]{1,0:T(4,128)(2,1)} %convert_element_type.264), channel_id=1, source_target_pairs={{32,0},{40,8},{48,16},{56,24},{64,32},{72,40},{80,48},{88,56},{96,... | collective-permute-start | bytes 6152 | tf_op jit(solution)/shard_map/ppermute | solution.py:17
  128.4 37.3 %collective-permute-start.12 = (bf16[4,256,128]{2,1,0:T(8,128)(2,1)}, bf16[4,256,128]{2,1,0:T(8,128)(2,1)S(1)}, u32[]{:S(2)}, u32[]{:S(2)}) collective-permute-start(bf16[4,256,128]{2,1,0:T(8,128)(2,1)} %get-tuple-element.2162), channel_id=1, source_target_pairs={{32,0},{40,8},{48,16},{56,24},{64,32},{72,40},{80,48},{88,56},{96,... | collective-permute-start | bytes 786440 | tf_op jit(solution)/shard_map/ppermute | solution.py:17
  135.9 50.0 %collective-permute-start.16 = (bf16[4,256]{1,0:T(4,128)(2,1)}, bf16[4,256]{1,0:T(4,128)(2,1)S(1)}, u32[]{:S(2)}, u32[]{:S(2)}) collective-permute-start(bf16[4,256]{1,0:T(4,128)(2,1)} %convert_element_type.264), channel_id=1, source_target_pairs={{24,0},{32,8},{40,16},{48,24},{56,32},{64,40},{72,48},{80,56},{88,... | collective-permute-start | bytes 6152 | tf_op jit(solution)/shard_map/ppermute | solution.py:17
  151.5 32.1 %collective-permute-start.15 = (bf16[4,256,128]{2,1,0:T(8,128)(2,1)}, bf16[4,256,128]{2,1,0:T(8,128)(2,1)S(1)}, u32[]{:S(2)}, u32[]{:S(2)}) collective-permute-start(bf16[4,256,128]{2,1,0:T(8,128)(2,1)} %get-tuple-element.2164), channel_id=1, source_target_pairs={{24,0},{32,8},{40,16},{48,24},{56,32},{64,40},{72,48},{80,56},{88,... | collective-permute-start | bytes 786440 | tf_op jit(solution)/shard_map/ppermute | solution.py:17
  154.2 41.7 %collective-permute-start.19 = (bf16[4,256]{1,0:T(4,128)(2,1)}, bf16[4,256]{1,0:T(4,128)(2,1)S(1)}, u32[]{:S(2)}, u32[]{:S(2)}) collective-permute-start(bf16[4,256]{1,0:T(4,128)(2,1)} %convert_element_type.264), channel_id=1, source_target_pairs={{16,0},{24,8},{32,16},{40,24},{48,32},{56,40},{64,48},{72,56},{80,... | collective-permute-start | bytes 6152 | tf_op jit(solution)/shard_map/ppermute | solution.py:17
  165.8 29.8 %collective-permute-start.18 = (bf16[4,256,128]{2,1,0:T(8,128)(2,1)}, bf16[4,256,128]{2,1,0:T(8,128)(2,1)S(1)}, u32[]{:S(2)}, u32[]{:S(2)}) collective-permute-start(bf16[4,256,128]{2,1,0:T(8,128)(2,1)} %get-tuple-element.2166), channel_id=1, source_target_pairs={{16,0},{24,8},{32,16},{40,24},{48,32},{56,40},{64,48},{72,56},{80,... | collective-permute-start | bytes 786440 | tf_op jit(solution)/shard_map/ppermute | solution.py:17
  170.8 35.9 %collective-permute-start.22 = (bf16[4,256]{1,0:T(4,128)(2,1)}, bf16[4,256]{1,0:T(4,128)(2,1)S(1)}, u32[]{:S(2)}, u32[]{:S(2)}) collective-permute-start(bf16[4,256]{1,0:T(4,128)(2,1)} %convert_element_type.264), channel_id=1, source_target_pairs={{8,0},{16,8},{24,16},{32,24},{40,32},{48,40},{56,48},{64,56},{72,6... | collective-permute-start | bytes 6152 | tf_op jit(solution)/shard_map/ppermute | solution.py:17
  183.6 21.9 %collective-permute-start.21 = (bf16[4,256,128]{2,1,0:T(8,128)(2,1)}, bf16[4,256,128]{2,1,0:T(8,128)(2,1)}, u32[]{:S(2)}, u32[]{:S(2)}) collective-permute-start(bf16[4,256,128]{2,1,0:T(8,128)(2,1)} %get-tuple-element.2168), channel_id=1, source_target_pairs={{8,0},{16,8},{24,16},{32,24},{40,32},{48,40},{56,48},{64,56},{72,6... | collective-permute-start | bytes 786440 | tf_op jit(solution)/shard_map/ppermute | solution.py:17
Sparse Core Ops, SparseCore 0:
  218.3 222.1 all-gather.2
